TPU v7x, 32 devices: a whole 2x2x4 slice. The times are simulated.
32 devices in a mesh: group: 2 (over y), exp: 4 (over z), tok: 4 (over x, core).
Axes of the slice: x: 2, y: 2, z: 4, core: 2. Of those that a mesh axis runs over, the one named last changes fastest.
Arguments:
- activations: bfloat16 [1024, 2048], P(('group', 'exp'), 'tok'), parts along dimension 0, may hold values from -6 to 6
- expert_ids: int32 [1024, 4], P(('group', 'exp')), parts along dimension 0, may hold values from 0 to 7, all different within a row; in each aligned block of 128 rows (0 to 127, 128 to 255, ...) at most 128 rows name the same one
- gate_values: float32 [1024, 4], P(('group', 'exp')), parts along dimension 0, may hold values from 0.2 to 1
- expert_gate: bfloat16 [8, 2048, 512], P('exp', 'tok'), may hold values from -0.125 to 0.125
- expert_up: bfloat16 [8, 2048, 512], P('exp', 'tok'), may hold values from -0.125 to 0.125
- expert_down: bfloat16 [8, 512, 2048], P('exp', None, 'tok'), may hold values from -0.25 to 0.25
Outputs:
- layer_out: bfloat16 [1024, 2048], P(('group', 'exp'), 'tok'), parts along dimension 0
There are 2 independent parts, one for each index of `group`. A program takes and returns all parts, laid end to end along the dimension named above; an argument that names none is the same for every part. Nothing has to cross between parts.
Inputs may be any that keep to these rules, and one draw needn't show every extreme that they name: `expert_ids`: each row names 4 different experts. Within each aligned block of 128 rows (the tokens of one index of exp) no expert is named by more than 128 rows, and in every draw some expert is named by exactly 128 rows of some block.
All inputs are finite; a program needn't handle non-finite values.
Results may differ from a plain program's by a relative error of at most 0.023.
Values may be sent and summed in bfloat16 or wider, within the bound.
A program may use at most 64 MiB of HBM per device.

v0:
```python
import jax
import jax.numpy as jnp
from jax import lax
from jax.sharding import PartitionSpec as P


def slot_positions(expert_ids, experts_all, capacity):
    flat_ids = expert_ids.reshape(-1)
    one_hot = (flat_ids[:, None] == jnp.arange(experts_all, dtype=jnp.int32)[None, :]).astype(
        jnp.int32
    )
    earlier = jnp.cumsum(one_hot, axis=0) - one_hot
    rank_within = jnp.sum(earlier * one_hot, axis=1)
    return flat_ids * capacity + rank_within


def move_rows(buffer):
    return lax.all_to_all(buffer, "exp", split_axis=0, concat_axis=0, tiled=True)


def shards(activations, expert_ids, gate_values, expert_gate, expert_up, expert_down):
    row_count, feature_cols = activations.shape
    top_count = expert_ids.shape[1]
    local_experts = expert_gate.shape[0]
    groups = lax.axis_size("exp")
    experts_all = local_experts * groups
    capacity = 2 * row_count * top_count // experts_all
    slot_index = slot_positions(expert_ids, experts_all, capacity)
    picked = jnp.repeat(activations, top_count, axis=0)
    outgoing = (
        jnp.zeros((experts_all * capacity, feature_cols), jnp.bfloat16).at[slot_index].set(picked)
    )
    arrived = move_rows(outgoing.reshape(groups, local_experts, capacity, feature_cols))
    gate_part = jnp.einsum(
        "sxcf,xfh->sxch", arrived, expert_gate, preferred_element_type=jnp.float32
    )
    up_part = jnp.einsum("sxcf,xfh->sxch", arrived, expert_up, preferred_element_type=jnp.float32)
    gate_pre, up_pre = (
        lax.psum(gate_part.astype(jnp.bfloat16), "tok").astype(jnp.float32),
        lax.psum(up_part.astype(jnp.bfloat16), "tok").astype(jnp.float32),
    )
    hidden = (jax.nn.silu(gate_pre) * up_pre).astype(jnp.bfloat16)
    results = jnp.einsum(
        "sxch,xhf->sxcf", hidden, expert_down, preferred_element_type=jnp.float32
    ).astype(jnp.bfloat16)
    returned = move_rows(results).reshape(experts_all * capacity, feature_cols)
    fetched = returned[slot_index].astype(jnp.float32).reshape(row_count, top_count, feature_cols)
    combined = jnp.sum(fetched * gate_values[:, :, None], axis=1)
    return combined.astype(jnp.bfloat16)


def solution(mesh):
    placed = (
        P(("group", "exp"), "tok"),
        P(("group", "exp"), None),
        P(("group", "exp"), None),
        P("exp", "tok", None),
        P("exp", "tok", None),
        P("exp", None, "tok"),
    )
    return jax.shard_map(
        shards, mesh=mesh, in_specs=placed, out_specs=P(("group", "exp"), "tok"), check_vma=False
    )
```

profile of v0, /device:TPU:0, one launch (start us, length us, event | category | flops | bytes accessed | tf_op | source)
XLA Modules:
  0.0 144.1 jit_solution(17230130679026216013)
XLA Ops:
  6.5 0.0 copy-start
  6.5 0.0 all-reduce.3.cloned.1.call-start
  6.5 0.9 copy.15
  7.4 0.1 eq.29
  7.5 0.1 eq.25
  7.6 0.7 broadcast_multiply_fusion
  8.3 1.1 reduce-window.6
  9.5 0.2 slice_reduce_fusion
  9.7 0.1 copy.14
  9.8 0.1 mul.36
  9.9 1.0 broadcast_in_dim.5
  11.0 0.1 reshape.77
  11.1 0.1 fusion.17
  11.2 2.7 %scatter_custom_fusion = bf16[1024,512]{1,0:T(8,128)(2,1)S(1)} fusion(s32[512]{0:T(512)S(1)} %bitcast.35, bf16[512,512]{1,0:T(8,128)(2,1)S(1)} %reshape.77, bf16[]{:T(256)} %constant.6.clone.1), kind=kCustom, calls=%fused_computation.21 | custom fusion | bytes 1048578 | tf_op jit(solution)/shard_map/scatter | solution.py:31
  14.0 31.9 %all_to_all.10 = bf16[4,2,128,512]{3,2,1,0:T(8,128)(2,1)S(1)} all-to-all(bf16[4,2,128,512]{3,2,1,0:T(8,128)(2,1)S(1)} %bitcast.34), channel_id=1, replica_groups=mesh['group'=2,'exp'=4,'tok'=4] {'exp'}, dimensions={0} | all-to-all | bytes 2097152 | tf_op jit(solution)/shard_map/all_to_all | solution.py:18
  45.8 0.0 copy-done
  45.8 0.0 copy-start.2
  45.8 1.7 %fusion.5 = bf16[4,2,128,512]{3,2,0,1:T(8,128)(2,1)} fusion(bf16[2,512,512]{2,1,0:T(8,128)(2,1)S(1)} %copy-done, bf16[4,2,128,512]{3,2,1,0:T(8,128)(2,1)S(1)} %all_to_all.10), kind=kOutput, calls=%fused_computation.12 | convolution fusion | flops 537395200 | bytes 3145728 | tf_op jit(solution)/shard_map/sxcf,xfh->sxch/dot_general | solution.py:34
  47.5 0.0 copy-done.2
  47.5 1.7 %fusion.6 = bf16[4,2,128,512]{3,2,0,1:T(8,128)(2,1)} fusion(bf16[2,512,512]{2,1,0:T(8,128)(2,1)S(1)} %copy-done.2, bf16[4,2,128,512]{3,2,1,0:T(8,128)(2,1)S(1)} %all_to_all.10), kind=kOutput, calls=%fused_computation.13 | convolution fusion | flops 537395200 | bytes 3145728 | tf_op jit(solution)/shard_map/sxcf,xfh->sxch/dot_general | solution.py:37
  49.2 0.0 copy-start.3
  49.2 0.0 all-reduce.3.cloned.1.call-update
  49.3 50.6 %all-reduce.3.cloned.1.call-done = (bf16[4,2,128,512]{3,2,0,1:T(8,128)(2,1)}, bf16[4,2,128,512]{3,2,0,1:T(8,128)(2,1)}) async-done(((bf16[4,2,128,512]{3,2,0,1:T(8,128)(2,1)}, bf16[4,2,128,512]{3,2,0,1:T(8,128)(2,1)}), (bf16[4,2,128,512]{3,2,0,1:T(8,128)(2,1)}, bf16[4,2,128,512]{3,2,0,1:T(8,128)(2,1)})) %all-reduce.3.cloned.1.call-update) | async-done | bytes 2097168 | tf_op jit(solution)/shard_map/psum | solution.py:40
  99.9 0.0 copy-done.3
  99.9 2.3 %fusion.7 = bf16[4,2,128,512]{3,2,0,1:T(8,128)(2,1)S(1)} fusion(bf16[2,512,512]{2,1,0:T(8,128)(2,1)S(1)} %copy-done.3, bf16[4,2,128,512]{3,2,0,1:T(8,128)(2,1)} %get-tuple-element.5, bf16[4,2,128,512]{3,2,0,1:T(8,128)(2,1)} %get-tuple-element.6), kind=kOutput, calls=%fused_computation.14 | convolution fusion | flops 541589504 | bytes 4194304 | tf_op jit(solution)/shard_map/sxch,xhf->sxcf/dot_general | solution.py:43
  102.3 1.1 copy.19
  103.4 0.0 copy-start.1
  103.4 4.7 %all-to-all-start.1 = ((bf16[4,2,128,512]{3,2,1,0:T(8,128)(2,1)}), bf16[4,2,128,512]{3,2,1,0:T(8,128)(2,1)S(1)}, u32[]{:S(2)}, u32[]{:S(2)}) async-start(bf16[4,2,128,512]{3,2,1,0:T(8,128)(2,1)} %copy.19), calls=%async_computation.1 | async-start | bytes 2097152 | tf_op jit(solution)/shard_map/all_to_all | solution.py:18
  108.1 0.0 copy-done.1
  108.1 0.1 copy.20
  108.2 25.4 %all-to-all-done.1 = bf16[4,2,128,512]{3,2,1,0:T(8,128)(2,1)S(1)} async-done(((bf16[4,2,128,512]{3,2,1,0:T(8,128)(2,1)}), bf16[4,2,128,512]{3,2,1,0:T(8,128)(2,1)S(1)}, u32[]{:S(2)}, u32[]{:S(2)}) %all-to-all-start.1) | async-done | bytes 1048608 | tf_op jit(solution)/shard_map/all_to_all | solution.py:18
  133.6 2.0 %gather_fusion = bf16[512,512]{1,0:T(8,128)(2,1)S(1)} fusion(bf16[1024,512]{1,0:T(8,128)(2,1)S(1)} %bitcast.33, s32[1024]{0:T(1024)S(1)} %pad_clamp_fusion), kind=kCustom, calls=%fused_computation | custom fusion | bytes 1050624 | tf_op jit(solution)/shard_map/gather | solution.py:47
  135.6 0.3 reshape.64
  135.9 1.4 multiply_reduce_fusion
  (5 shorter events, 0.1 us)
Async XLA Ops:
  6.5 39.3 %copy-start = (bf16[2,512,512]{2,1,0:T(8,128)(2,1)S(1)}, bf16[2,512,512]{2,1,0:T(8,128)(2,1)}, u32[]{:S(2)}) copy-start(bf16[2,512,512]{2,1,0:T(8,128)(2,1)} %param.9) | copy-start | bytes 3145732
  6.5 93.4 %all-reduce.3.cloned.1.call-start = ((), (), s32[]{:S(2)}) async-start(), calls=%async_computation.2 | async-start | bytes 4194304 | tf_op jit(solution)/shard_map/psum | solution.py:40
  45.8 1.7 %copy-start.2 = (bf16[2,512,512]{2,1,0:T(8,128)(2,1)S(1)}, bf16[2,512,512]{2,1,0:T(8,128)(2,1)}, u32[]{:S(2)}) copy-start(bf16[2,512,512]{2,1,0:T(8,128)(2,1)} %param.10) | copy-start | bytes 3145732
  49.2 50.7 %copy-start.3 = (bf16[2,512,512]{2,1,0:T(8,128)(2,1)S(1)}, bf16[2,512,512]{2,1,0:T(8,128)(2,1)}, u32[]{:S(2)}) copy-start(bf16[2,512,512]{2,1,0:T(8,128)(2,1)} %param.11) | copy-start | bytes 3145732
  103.4 4.7 %copy-start.1 = (f32[128,4]{0,1:T(4,128)S(1)}, f32[128,4]{0,1:T(4,128)}, u32[]{:S(2)}) copy-start(f32[128,4]{0,1:T(4,128)} %param.8) | copy-start | bytes 6148
  103.4 30.2 %all-to-all-start.1 = ((bf16[4,2,128,512]{3,2,1,0:T(8,128)(2,1)}), bf16[4,2,128,512]{3,2,1,0:T(8,128)(2,1)S(1)}, u32[]{:S(2)}, u32[]{:S(2)}) async-start(bf16[4,2,128,512]{3,2,1,0:T(8,128)(2,1)} %copy.19), calls=%async_computation.1 | async-start | bytes 2097152 | tf_op jit(solution)/shard_map/all_to_all | solution.py:18
Sparse Core Ops, SparseCore 0:
  49.4 50.4 all-reduce.2
where the time goes:
time: 144 us
  waiting for transfers between devices  76 us (53%)
  blocking collectives  31.9 us (22%)
  between operations  13.4 us (9%)
  local copies, waits for them, and re-layouts  8.96 us (6%)
  matrix products  5.73 us (4%)
  starting transfers between devices  4.73 us (3%)
  other arithmetic  3.33 us (2%)
    psum x1, waiting for transfers between devices, shards(): lax.psum(up_part.astype(jnp.bfloat16), 'tok').astype(jnp.float32)  50.6 us
    all_to_all x1, blocking collectives, move_rows(): lax.all_to_all(buffer, 'exp', split_axis=0, concat_axis=0, tiled=True)  31.9 us
    all_to_all x1, waiting for transfers between devices, move_rows(): lax.all_to_all(buffer, 'exp', split_axis=0, concat_axis=0, tiled=True)  25.4 us
    all_to_all x1, starting transfers between devices, move_rows(): lax.all_to_all(buffer, 'exp', split_axis=0, concat_axis=0, tiled=True)  4.73 us
  transfers between devices with their start and end apart: 2, of which 2 were waited for; matrix products, arithmetic and copies ran while one was open for 0% of the time, Pallas kernels for 0%

commit v1 on v0

--- a/solution.py
+++ b/solution.py
@@ -1,7 +1,13 @@
+import functools
+
 import jax
 import jax.numpy as jnp
 from jax import lax
+from jax.experimental import pallas as pl
+from jax.experimental.pallas import tpu as pltpu
 from jax.sharding import PartitionSpec as P
+
+MESH = pl.DeviceIdType.MESH
 
 
 def slot_positions(expert_ids, experts_all, capacity):
@@ -18,7 +24,7 @@
     return lax.all_to_all(buffer, "exp", split_axis=0, concat_axis=0, tiled=True)
 
 
-def shards(activations, expert_ids, gate_values, expert_gate, expert_up, expert_down):
+def slot_layer(activations, expert_ids, gate_values, expert_gate, expert_up, expert_down):
     row_count, feature_cols = activations.shape
     top_count = expert_ids.shape[1]
     local_experts = expert_gate.shape[0]
@@ -49,6 +55,272 @@
     return combined.astype(jnp.bfloat16)
 
 
+def block_order(n):
+    return [sorted(range(n), key=lambda b: (abs(b - i), b)) for i in range(n)]
+
+
+def skewed(n, stages):
+    for tick in range(n + stages - 1):
+        for stage in range(stages):
+            if 0 <= tick - stage < n:
+                yield stage, tick - stage
+
+
+def dense_kernel(
+    n, ids_ref, gv_ref, a_ref, wg_hbm, wu_hbm, wd_hbm, out_ref,
+    wg, wu, wd, gates, xg, keep, csend, crecv, mine, xsend, xrecv, hid, outb, ret, acc,
+    w_sem, z_send, z_recv, g_send, g_recv, c_send, c_recv, x_send, x_recv, h_send, h_recv,
+    r_send, r_recv,
+):
+    rows = a_ref.shape[0]
+    local_experts, _, ff = wg.shape
+    half, quarter = rows // 2, rows // 4
+    me, t = lax.axis_index("exp"), lax.axis_index("tok")
+    c, xx = lax.rem(t, 2), lax.div(t, 2)
+    core_peer, chip_peer = {"tok": xx * 2 + 1 - c}, {"tok": (1 - xx) * 2 + c}
+    own_q, chip_q = c * 2 + xx, c * 2 + 1 - xx
+    table = block_order(n)
+
+    def block(step):
+        b = me * 0
+        for i in range(n):
+            b = jnp.where(me == i, table[i][step], b)
+        return b
+
+    def send(src, dst, ss, rs, where):
+        return pltpu.make_async_remote_copy(
+            src_ref=src, dst_ref=dst, send_sem=ss, recv_sem=rs, device_id=where, device_id_type=MESH
+        )
+
+    weights = [
+        pltpu.make_async_copy(src, dst, w_sem.at[i])
+        for i, (src, dst) in enumerate(((wg_hbm, wg), (wu_hbm, wu), (wd_hbm, wd)))
+    ]
+    for copy in weights:
+        copy.start()
+
+    barrier = pltpu.get_barrier_semaphore()
+    for j in range(1, n):
+        pl.semaphore_signal(
+            barrier, inc=1, device_id={"exp": lax.rem(me + j, n)}, device_id_type=MESH
+        )
+    for peer in (core_peer, chip_peer):
+        pl.semaphore_signal(barrier, inc=1, device_id=peer, device_id_type=MESH)
+
+    row0 = pl.multiple_of(own_q * quarter, quarter)
+    ids, values = ids_ref[pl.ds(row0, quarter), :], gv_ref[pl.ds(row0, quarter), :]
+    lanes = lax.broadcasted_iota(jnp.int32, gates.shape[1:], 1)
+    table_of_gates = jnp.zeros(gates.shape[1:], jnp.float32)
+    for k in range(ids.shape[1]):
+        table_of_gates += jnp.where(lanes == ids[:, k : k + 1], values[:, k : k + 1], 0.0)
+    gates[me] = table_of_gates
+    pl.semaphore_wait(barrier, n + 1)
+
+    def pass_on(b, src):
+        return (
+            (
+                jnp.logical_and(b <= me, me < n - 1),
+                send(src, xg.at[b], z_send.at[0, b], z_recv.at[b], {"exp": lax.rem(me + 1, n)}),
+            ),
+            (
+                jnp.logical_and(b >= me, me > 0),
+                send(src, xg.at[b], z_send.at[1, b], z_recv.at[b], {"exp": lax.rem(me + n - 1, n)}),
+            ),
+        )
+
+    def start(copies):
+        for condition, copy in copies:
+            pl.when(condition)(copy.start)
+
+    start(pass_on(me, a_ref))
+    gate_copies = [
+        send(gates.at[me], gates.at[me], g_send.at[j], g_recv.at[me], {"exp": lax.rem(me + j, n)})
+        for j in range(1, n)
+    ]
+    for copy in gate_copies:
+        copy.start()
+    weights[0].wait()
+    weights[1].wait()
+
+    def to_core(s):
+        return send(csend.at[s], crecv.at[s], c_send.at[s], c_recv.at[s], core_peer)
+
+    def to_chip(s):
+        return send(xsend.at[s], xrecv.at[s], x_send.at[s], x_recv.at[s], chip_peer)
+
+    def hidden_copy(s, kind):
+        q = (own_q, own_q, chip_q)[kind]
+        peer = (chip_peer, core_peer, core_peer)[kind]
+        return send(
+            hid.at[s, q], hid.at[s, q], h_send.at[s, kind], h_recv.at[s, kind], peer
+        )
+
+    def hidden_arrival(s, kind):
+        q = (chip_q, (1 - c) * 2 + xx, (1 - c) * 2 + 1 - xx)[kind]
+        peer = (chip_peer, core_peer, core_peer)[kind]
+        return send(
+            hid.at[s, q], hid.at[s, q], h_send.at[s, kind], h_recv.at[s, kind], peer
+        )
+
+    def result_copy(s):
+        b = block(s)
+        return send(outb.at[s], ret.at[me], r_send.at[s], r_recv.at[me], {"exp": b})
+
+    def partial(s):
+        b = block(s)
+        if s > 0:
+            send(
+                xg.at[b], xg.at[b], z_send.at[0, b], z_recv.at[b], {"exp": lax.rem(me + 1, n)}
+            ).wait_recv()
+            start(pass_on(b, xg.at[b]))
+        first = pl.ds(pl.multiple_of(c * half, half), half)
+        second = pl.ds(pl.multiple_of((1 - c) * half, half), half)
+        if s == 0:
+            block_rows = jnp.concatenate([a_ref[first, :], a_ref[second, :]], axis=0)
+        else:
+            block_rows = jnp.concatenate([xg[b, first, :], xg[b, second, :]], axis=0)
+        for e in range(local_experts):
+            for i, w in enumerate((wg, wu)):
+                part = jnp.dot(block_rows, w[e], preferred_element_type=jnp.float32)
+                cols = pl.ds((2 * e + i) * ff, ff)
+                csend[s, :, cols] = part[half:].astype(jnp.bfloat16)
+                keep[s, :, cols] = part[:half]
+        to_core(s).start()
+
+    def chip_sum(s):
+        to_core(s).wait_recv()
+        own = pl.ds(pl.multiple_of(xx * quarter, quarter), quarter)
+        other = pl.ds(pl.multiple_of((1 - xx) * quarter, quarter), quarter)
+        xsend[s] = (keep[s, other, :] + crecv[s, other, :].astype(jnp.float32)).astype(jnp.bfloat16)
+        to_chip(s).start()
+        mine[s] = keep[s, own, :] + crecv[s, own, :].astype(jnp.float32)
+
+    def activate(s):
+        b = block(s)
+        if s > 0:
+            send(
+                gates.at[b], gates.at[b], g_send.at[s], g_recv.at[b], {"exp": lax.rem(me + 1, n)}
+            ).wait_recv()
+        to_chip(s).wait_recv()
+        weight_of = gates[b]
+        for e in range(local_experts):
+            gate_cols, up_cols = pl.ds(2 * e * ff, ff), pl.ds((2 * e + 1) * ff, ff)
+            g = mine[s, :, gate_cols] + xrecv[s, :, gate_cols].astype(jnp.float32)
+            u = mine[s, :, up_cols] + xrecv[s, :, up_cols].astype(jnp.float32)
+            scale = jnp.sum(
+                jnp.where(lanes == me * local_experts + e, weight_of, 0.0), axis=1, keepdims=True
+            )
+            hid[s, own_q, :, pl.ds(e * ff, ff)] = (g / (1.0 + jnp.exp(-g)) * (u * scale)).astype(
+                jnp.bfloat16
+            )
+        hidden_copy(s, 0).start()
+        hidden_copy(s, 1).start()
+
+    def hand_on(s):
+        hidden_arrival(s, 0).wait_recv()
+        hidden_copy(s, 2).start()
+
+    def project(s):
+        hidden_arrival(s, 1).wait_recv()
+        hidden_arrival(s, 2).wait_recv()
+        if s == 0:
+            weights[2].wait()
+        h = hid[s].reshape(rows, local_experts * ff)
+        result = jnp.dot(
+            h, wd[...].reshape(local_experts * ff, wd.shape[2]), preferred_element_type=jnp.float32
+        )
+        if s == 0:
+            acc[...] = result
+        else:
+            outb[s] = result.astype(jnp.bfloat16)
+            result_copy(s).start()
+
+    stages = (partial, chip_sum, activate, hand_on, project)
+    for stage, s in skewed(n, len(stages)):
+        stages[stage](s)
+
+    total = acc[...]
+    for s in range(1, n):
+        b = block(s)
+        send(
+            outb.at[s], ret.at[b], r_send.at[s], r_recv.at[b], {"exp": b}
+        ).wait_recv()
+        total += ret[b].astype(jnp.float32)
+    out_ref[...] = total.astype(out_ref.dtype)
+
+    for s in range(n):
+        b = block(s)
+        for condition, copy in pass_on(b, a_ref if s == 0 else xg.at[b]):
+            pl.when(condition)(copy.wait_send)
+        to_core(s).wait_send()
+        to_chip(s).wait_send()
+        for kind in range(3):
+            hidden_copy(s, kind).wait_send()
+        if s > 0:
+            result_copy(s).wait_send()
+    for copy in gate_copies:
+        copy.wait_send()
+
+
+def dense_layer(activations, expert_ids, gate_values, expert_gate, expert_up, expert_down):
+    n = lax.axis_size("exp")
+    rows, cols = activations.shape
+    local_experts, _, ff = expert_gate.shape
+    wide, joined = 2 * local_experts * ff, local_experts * ff
+    half, quarter = rows // 2, rows // 4
+    lanes = -(-local_experts * n // 128) * 128
+    bf16, f32 = jnp.bfloat16, jnp.float32
+    vmem, hbm = pl.BlockSpec(memory_space=pltpu.VMEM), pl.BlockSpec(memory_space=pl.ANY)
+    dma = pltpu.SemaphoreType.DMA
+    return pl.pallas_call(
+        functools.partial(dense_kernel, n),
+        out_shape=jax.ShapeDtypeStruct((rows, cols), bf16),
+        in_specs=[vmem, vmem, vmem, hbm, hbm, hbm],
+        out_specs=vmem,
+        scratch_shapes=[
+            pltpu.VMEM(expert_gate.shape, bf16),
+            pltpu.VMEM(expert_up.shape, bf16),
+            pltpu.VMEM(expert_down.shape, bf16),
+            pltpu.VMEM((n, quarter, lanes), f32),
+            pltpu.VMEM((n, rows, cols), bf16),
+            pltpu.VMEM((n, half, wide), f32),
+            pltpu.VMEM((n, half, wide), bf16),
+            pltpu.VMEM((n, half, wide), bf16),
+            pltpu.VMEM((n, quarter, wide), f32),
+            pltpu.VMEM((n, quarter, wide), bf16),
+            pltpu.VMEM((n, quarter, wide), bf16),
+            pltpu.VMEM((n, 4, quarter, joined), bf16),
+            pltpu.VMEM((n, rows, cols), bf16),
+            pltpu.VMEM((n, rows, cols), bf16),
+            pltpu.VMEM((rows, cols), f32),
+            dma((3,)),
+            dma((2, n)),
+            dma((n,)),
+            dma((n,)),
+            dma((n,)),
+            dma((n,)),
+            dma((n,)),
+            dma((n,)),
+            dma((n,)),
+            dma((n, 3)),
+            dma((n, 3)),
+            dma((n,)),
+            dma((n,)),
+        ],
+        compiler_params=pltpu.CompilerParams(
+            collective_id=0, has_side_effects=True, vmem_limit_bytes=48 * 1024 * 1024
+        ),
+    )(expert_ids, gate_values, activations, expert_gate, expert_up, expert_down)
+
+
+def shards(activations, expert_ids, gate_values, expert_gate, expert_up, expert_down):
+    rows = activations.shape[0]
+    experts_all = expert_gate.shape[0] * lax.axis_size("exp")
+    capacity = 2 * rows * expert_ids.shape[1] // experts_all
+    layer = dense_layer if capacity >= rows and lax.axis_size("tok") == 4 else slot_layer
+    return layer(activations, expert_ids, gate_values, expert_gate, expert_up, expert_down)
+
+
 def solution(mesh):
     placed = (
         P(("group", "exp"), "tok"),

time: 144 us -> 47.3 us (0.33)
  waiting for transfers between devices: 76 us -> 0 us
  Pallas kernels: 0 us -> 41.8 us
  blocking collectives: 31.9 us -> 0 us
  between operations: 13.4 us -> 0.03 us
  matrix products: 5.73 us -> 0 us
  starting transfers between devices: 4.73 us -> 0 us
  local copies, waits for them, and re-layouts: 8.96 us -> 5.27 us
  other arithmetic: 3.33 us -> 0 us
    psum x1 -> x0, waiting for transfers between devices: 50.6 us -> none  [shards(): lax.psum(up_part.astype(jnp.bfloat16), 'tok').astype(jnp.float32)]
    pallas_call x0 -> x1, Pallas kernels: none -> 41.8 us  [dense_layer(): pl.pallas_call(functools.partial(dense_kernel, n), out_shape=jax.ShapeDty...]
    all_to_all x1 -> x0, blocking collectives: 31.9 us -> none  [move_rows(): lax.all_to_all(buffer, 'exp', split_axis=0, concat_axis=0, tiled=True)]
    all_to_all x1 -> x0, waiting for transfers between devices: 25.4 us -> none  [move_rows(): lax.all_to_all(buffer, 'exp', split_axis=0, concat_axis=0, tiled=True)]
    dot_general x3 -> x0, matrix products: 5.73 us -> none  [the longest x1 2.33 us: shards(): jnp.einsum('sxch,xhf->sxcf', hidden, expert_down, preferred_element_type=...]
    all_to_all x1 -> x0, starting transfers between devices: 4.73 us -> none  [move_rows(): lax.all_to_all(buffer, 'exp', split_axis=0, concat_axis=0, tiled=True)]
    unnamed x10 -> x13, local copies, waits for them, and re-layouts: 1 us -> 5.27 us
    scatter x1 -> x0, local copies, waits for them, and re-layouts: 2.74 us -> none  [shards(): jnp.zeros((experts_all * capacity, feature_cols), jnp.bfloat16)]
  transfers between devices with their start and end apart: 2 -> 0, of which waited for: 2 -> 0; matrix products, arithmetic and copies ran while one was open for 0% -> 0% of each run, Pallas kernels for 0% -> 0%
where the time goes in v1:
time: 47.3 us; the launch traced here: 47.1 us
  Pallas kernels  41.8 us (88%)
  local copies, waits for them, and re-layouts  5.27 us (11%)
    pallas_call x1, Pallas kernels, dense_layer(): pl.pallas_call(functools.partial(dense_kernel, n), out_shape=jax.ShapeDty...  41.8 us
    unnamed x13, local copies, waits for them, and re-layouts  5.27 us

profile of v1, /device:TPU:0, one launch (start us, length us, event | category | flops | bytes accessed | tf_op | source)
XLA Modules:
  0.0 47.1 jit_solution(7862799499218238713)
XLA Ops:
  0.0 0.0 copy-start.4
  0.0 0.0 copy-start.3
  0.0 0.8 %copy.7.ids_ref = s32[128,4]{1,0:T(8,128)S(1)} copy(s32[128,4]{0,1:T(4,128)} %param.7) | data formatting | bytes 4096 | tf_op args[1]
  0.8 0.0 copy-done.4
  0.8 0.1 copy.8.gv_ref
  0.9 0.0 copy-done.3
  0.9 0.0 copy-start
  1.0 1.2 %copy-done = bf16[2,512,512]{2,1,0:T(8,128)(2,1)S(1)} copy-done((bf16[2,512,512]{2,1,0:T(8,128)(2,1)S(1)}, bf16[2,512,512]{2,1,0:T(8,128)(2,1)}, u32[]{:S(2)}) %copy-start) | copy-done | bytes 1048600
  2.2 0.0 copy-start.1
  2.2 1.2 %copy-done.1 = bf16[2,512,512]{2,1,0:T(8,128)(2,1)S(1)} copy-done((bf16[2,512,512]{2,1,0:T(8,128)(2,1)S(1)}, bf16[2,512,512]{2,1,0:T(8,128)(2,1)}, u32[]{:S(2)}) %copy-start.1) | copy-done | bytes 1048600
  3.4 0.0 copy-start.2
  3.4 1.2 %copy-done.2 = bf16[2,512,512]{2,1,0:T(8,128)(2,1)S(1)} copy-done((bf16[2,512,512]{2,1,0:T(8,128)(2,1)S(1)}, bf16[2,512,512]{2,1,0:T(8,128)(2,1)}, u32[]{:S(2)}) %copy-start.2) | copy-done | bytes 1048600
  4.6 41.8 %shard_map.64 = bf16[128,512]{1,0:T(8,128)(2,1)S(1)} custom-call(s32[128,4]{1,0:T(8,128)S(1)} %copy.7.ids_ref, f32[128,4]{1,0:T(8,128)S(1)} %copy.8.gv_ref, bf16[128,512]{1,0:T(8,128)(2,1)S(1)} %copy-done.3, bf16[2,512,512]{2,1,0:T(8,128)(2,1)S(1)} %copy-done, bf16[2,512,512]{2,1,0:T(8,128)(2,1)S(1)} %copy-done.1, bf16[2,512,512]{2,1,0:T(8,128)(2,1)S(1)} %copy-done.2), custom_call_target="tpu_custom_call" | custom-call | tf_op jit(solution)/shard_map/pallas_call | solution.py:275
  46.4 0.7 %copy.10 = bf16[128,512]{1,0:T(8,128)(2,1)} copy(bf16[128,512]{1,0:T(8,128)(2,1)S(1)} %shard_map.64) | data formatting | bytes 262144
Async XLA Ops:
  0.0 0.8 %copy-start.4 = (f32[128,4]{0,1:T(4,128)S(1)}, f32[128,4]{0,1:T(4,128)}, u32[]{:S(2)}) copy-start(f32[128,4]{0,1:T(4,128)} %param.8) | copy-start | bytes 6148
  0.0 0.9 %copy-start.3 = (bf16[128,512]{1,0:T(8,128)(2,1)S(1)}, bf16[128,512]{1,0:T(8,128)(2,1)}, u32[]{:S(2)}) copy-start(bf16[128,512]{1,0:T(8,128)(2,1)} %a_ref.1) | copy-start | bytes 393220
  0.9 1.2 %copy-start = (bf16[2,512,512]{2,1,0:T(8,128)(2,1)S(1)}, bf16[2,512,512]{2,1,0:T(8,128)(2,1)}, u32[]{:S(2)}) copy-start(bf16[2,512,512]{2,1,0:T(8,128)(2,1)} %wg_hbm.1) | copy-start | bytes 3145732
  2.2 1.2 %copy-start.1 = (bf16[2,512,512]{2,1,0:T(8,128)(2,1)S(1)}, bf16[2,512,512]{2,1,0:T(8,128)(2,1)}, u32[]{:S(2)}) copy-start(bf16[2,512,512]{2,1,0:T(8,128)(2,1)} %wu_hbm.1) | copy-start | bytes 3145732
  3.4 1.2 %copy-start.2 = (bf16[2,512,512]{2,1,0:T(8,128)(2,1)S(1)}, bf16[2,512,512]{2,1,0:T(8,128)(2,1)}, u32[]{:S(2)}) copy-start(bf16[2,512,512]{2,1,0:T(8,128)(2,1)} %wd_hbm.1) | copy-start | bytes 3145732

commit v2 on v1

--- a/solution.py
+++ b/solution.py
@@ -59,20 +59,26 @@
     return [sorted(range(n), key=lambda b: (abs(b - i), b)) for i in range(n)]
 
 
-def skewed(n, stages):
-    for tick in range(n + stages - 1):
-        for stage in range(stages):
-            if 0 <= tick - stage < n:
-                yield stage, tick - stage
+def run_order(n):
+    if n < 4:
+        return [(k, s) for k in "ABCDE" for s in range(n) if (k, s) != ("A", 0)]
+    last, middle = n - 1, range(1, n - 2)
+    plan = [("B", 0)]
+    plan += [(k, s) for s in range(1, last) for k in "AB"]
+    plan += [("C", s) for s in range(n - 2)]
+    plan += [("A", last), ("B", last)]
+    plan += [("D", s) for s in middle] + [("C", n - 2), ("D", 0)] + [("E", s) for s in middle]
+    plan += [("C", last), ("D", n - 2), ("E", n - 2), ("E", 0), ("D", last), ("E", last)]
+    return plan
 
 
 def dense_kernel(
-    n, ids_ref, gv_ref, a_ref, wg_hbm, wu_hbm, wd_hbm, out_ref,
-    wg, wu, wd, gates, xg, keep, csend, crecv, mine, xsend, xrecv, hid, outb, ret, acc,
+    n, ids_hbm, gv_hbm, a_hbm, wg_hbm, wu_hbm, wd_hbm, out_ref,
+    ids_ref, gv_ref, wg, wu, wd, gates, xg, keep, csend, crecv, mine, xsend, xrecv, hid, outb, ret, acc,
     w_sem, z_send, z_recv, g_send, g_recv, c_send, c_recv, x_send, x_recv, h_send, h_recv,
     r_send, r_recv,
 ):
-    rows = a_ref.shape[0]
+    rows = xg.shape[1]
     local_experts, _, ff = wg.shape
     half, quarter = rows // 2, rows // 4
     me, t = lax.axis_index("exp"), lax.axis_index("tok")
@@ -92,11 +98,20 @@
             src_ref=src, dst_ref=dst, send_sem=ss, recv_sem=rs, device_id=where, device_id_type=MESH
         )
 
-    weights = [
+    loads = [
         pltpu.make_async_copy(src, dst, w_sem.at[i])
-        for i, (src, dst) in enumerate(((wg_hbm, wg), (wu_hbm, wu), (wd_hbm, wd)))
+        for i, (src, dst) in enumerate(
+            (
+                (a_hbm, xg.at[me]),
+                (wg_hbm, wg),
+                (wu_hbm, wu),
+                (ids_hbm, ids_ref),
+                (gv_hbm, gv_ref),
+                (wd_hbm, wd),
+            )
+        )
     ]
-    for copy in weights:
+    for copy in loads:
         copy.start()
 
     barrier = pltpu.get_barrier_semaphore()
@@ -107,40 +122,19 @@
     for peer in (core_peer, chip_peer):
         pl.semaphore_signal(barrier, inc=1, device_id=peer, device_id_type=MESH)
 
-    row0 = pl.multiple_of(own_q * quarter, quarter)
-    ids, values = ids_ref[pl.ds(row0, quarter), :], gv_ref[pl.ds(row0, quarter), :]
-    lanes = lax.broadcasted_iota(jnp.int32, gates.shape[1:], 1)
-    table_of_gates = jnp.zeros(gates.shape[1:], jnp.float32)
-    for k in range(ids.shape[1]):
-        table_of_gates += jnp.where(lanes == ids[:, k : k + 1], values[:, k : k + 1], 0.0)
-    gates[me] = table_of_gates
-    pl.semaphore_wait(barrier, n + 1)
-
-    def pass_on(b, src):
-        return (
+    def spread(buffer, send_sem, recv_sem):
+        return [
             (
-                jnp.logical_and(b <= me, me < n - 1),
-                send(src, xg.at[b], z_send.at[0, b], z_recv.at[b], {"exp": lax.rem(me + 1, n)}),
-            ),
-            (
-                jnp.logical_and(b >= me, me > 0),
-                send(src, xg.at[b], z_send.at[1, b], z_recv.at[b], {"exp": lax.rem(me + n - 1, n)}),
-            ),
-        )
-
-    def start(copies):
-        for condition, copy in copies:
-            pl.when(condition)(copy.start)
-
-    start(pass_on(me, a_ref))
-    gate_copies = [
-        send(gates.at[me], gates.at[me], g_send.at[j], g_recv.at[me], {"exp": lax.rem(me + j, n)})
-        for j in range(1, n)
-    ]
-    for copy in gate_copies:
-        copy.start()
-    weights[0].wait()
-    weights[1].wait()
+                jnp.logical_and(peer >= 0, peer < n),
+                send(
+                    buffer.at[me], buffer.at[me], send_sem.at[i], recv_sem.at[me],
+                    {"exp": jnp.clip(peer, 0, n - 1)},
+                ),
+            )
+            for i, peer in enumerate(me + d * sign for d in range(1, n) for sign in (1, -1))
+        ]
+
+    row_copies, gate_copies = spread(xg, z_send, z_recv), spread(gates, g_send, g_recv)
 
     def to_core(s):
         return send(csend.at[s], crecv.at[s], c_send.at[s], c_recv.at[s], core_peer)
@@ -170,22 +164,19 @@
         b = block(s)
         if s > 0:
             send(
-                xg.at[b], xg.at[b], z_send.at[0, b], z_recv.at[b], {"exp": lax.rem(me + 1, n)}
+                xg.at[b], xg.at[b], z_send.at[0], z_recv.at[b], {"exp": lax.rem(me + 1, n)}
             ).wait_recv()
-            start(pass_on(b, xg.at[b]))
         first = pl.ds(pl.multiple_of(c * half, half), half)
         second = pl.ds(pl.multiple_of((1 - c) * half, half), half)
-        if s == 0:
-            block_rows = jnp.concatenate([a_ref[first, :], a_ref[second, :]], axis=0)
-        else:
-            block_rows = jnp.concatenate([xg[b, first, :], xg[b, second, :]], axis=0)
+        block_rows = jnp.concatenate([xg[b, first, :], xg[b, second, :]], axis=0)
         for e in range(local_experts):
             for i, w in enumerate((wg, wu)):
                 part = jnp.dot(block_rows, w[e], preferred_element_type=jnp.float32)
                 cols = pl.ds((2 * e + i) * ff, ff)
                 csend[s, :, cols] = part[half:].astype(jnp.bfloat16)
                 keep[s, :, cols] = part[:half]
-        to_core(s).start()
+        if s > 0:
+            to_core(s).start()
 
     def chip_sum(s):
         to_core(s).wait_recv()
@@ -199,17 +190,19 @@
         b = block(s)
         if s > 0:
             send(
-                gates.at[b], gates.at[b], g_send.at[s], g_recv.at[b], {"exp": lax.rem(me + 1, n)}
+                gates.at[b], gates.at[b], g_send.at[0], g_recv.at[b], {"exp": lax.rem(me + 1, n)}
             ).wait_recv()
         to_chip(s).wait_recv()
-        weight_of = gates[b]
+        square = (quarter, rows)
+        diagonal = lax.broadcasted_iota(jnp.int32, square, 1) == (
+            own_q * quarter + lax.broadcasted_iota(jnp.int32, square, 0)
+        )
         for e in range(local_experts):
             gate_cols, up_cols = pl.ds(2 * e * ff, ff), pl.ds((2 * e + 1) * ff, ff)
             g = mine[s, :, gate_cols] + xrecv[s, :, gate_cols].astype(jnp.float32)
             u = mine[s, :, up_cols] + xrecv[s, :, up_cols].astype(jnp.float32)
-            scale = jnp.sum(
-                jnp.where(lanes == me * local_experts + e, weight_of, 0.0), axis=1, keepdims=True
-            )
+            weight_of = gates[b, pl.ds(me * local_experts + e, 1), :]
+            scale = jnp.sum(jnp.where(diagonal, weight_of, 0.0), axis=1, keepdims=True)
             hid[s, own_q, :, pl.ds(e * ff, ff)] = (g / (1.0 + jnp.exp(-g)) * (u * scale)).astype(
                 jnp.bfloat16
             )
@@ -223,8 +216,8 @@
     def project(s):
         hidden_arrival(s, 1).wait_recv()
         hidden_arrival(s, 2).wait_recv()
-        if s == 0:
-            weights[2].wait()
+        if s == first_projected:
+            loads[5].wait()
         h = hid[s].reshape(rows, local_experts * ff)
         result = jnp.dot(
             h, wd[...].reshape(local_experts * ff, wd.shape[2]), preferred_element_type=jnp.float32
@@ -235,8 +228,25 @@
             outb[s] = result.astype(jnp.bfloat16)
             result_copy(s).start()
 
-    stages = (partial, chip_sum, activate, hand_on, project)
-    for stage, s in skewed(n, len(stages)):
+    stages = {"A": partial, "B": chip_sum, "C": activate, "D": hand_on, "E": project}
+    plan = run_order(n)
+    first_projected = next(s for stage, s in plan if stage == "E")
+
+    for copy in loads[:3]:
+        copy.wait()
+    partial(0)
+    for copy in loads[3:5]:
+        copy.wait()
+    experts = lax.broadcasted_iota(jnp.int32, gates.shape[1:], 0)
+    table_of_gates = jnp.zeros(gates.shape[1:], jnp.float32)
+    for k in range(ids_ref.shape[0]):
+        table_of_gates += jnp.where(experts == ids_ref[k : k + 1, :], gv_ref[k : k + 1, :], 0.0)
+    gates[me] = table_of_gates
+    pl.semaphore_wait(barrier, n + 1)
+    to_core(0).start()
+    for condition, copy in row_copies + gate_copies:
+        pl.when(condition)(copy.start)
+    for stage, s in plan:
         stages[stage](s)
 
     total = acc[...]
@@ -249,17 +259,14 @@
     out_ref[...] = total.astype(out_ref.dtype)
 
     for s in range(n):
-        b = block(s)
-        for condition, copy in pass_on(b, a_ref if s == 0 else xg.at[b]):
-            pl.when(condition)(copy.wait_send)
         to_core(s).wait_send()
         to_chip(s).wait_send()
         for kind in range(3):
             hidden_copy(s, kind).wait_send()
         if s > 0:
             result_copy(s).wait_send()
-    for copy in gate_copies:
-        copy.wait_send()
+    for condition, copy in row_copies + gate_copies:
+        pl.when(condition)(copy.wait_send)
 
 
 def dense_layer(activations, expert_ids, gate_values, expert_gate, expert_up, expert_down):
@@ -268,20 +275,23 @@
     local_experts, _, ff = expert_gate.shape
     wide, joined = 2 * local_experts * ff, local_experts * ff
     half, quarter = rows // 2, rows // 4
-    lanes = -(-local_experts * n // 128) * 128
+    experts = -(-local_experts * n // 8) * 8
+    top = expert_ids.shape[1]
     bf16, f32 = jnp.bfloat16, jnp.float32
-    vmem, hbm = pl.BlockSpec(memory_space=pltpu.VMEM), pl.BlockSpec(memory_space=pl.ANY)
+    vmem, hbm = pl.BlockSpec(memory_space=pltpu.VMEM), pl.BlockSpec(memory_space=pltpu.HBM)
     dma = pltpu.SemaphoreType.DMA
     return pl.pallas_call(
         functools.partial(dense_kernel, n),
         out_shape=jax.ShapeDtypeStruct((rows, cols), bf16),
-        in_specs=[vmem, vmem, vmem, hbm, hbm, hbm],
+        in_specs=[hbm] * 6,
         out_specs=vmem,
         scratch_shapes=[
+            pltpu.VMEM((top, rows), jnp.int32),
+            pltpu.VMEM((top, rows), f32),
             pltpu.VMEM(expert_gate.shape, bf16),
             pltpu.VMEM(expert_up.shape, bf16),
             pltpu.VMEM(expert_down.shape, bf16),
-            pltpu.VMEM((n, quarter, lanes), f32),
+            pltpu.VMEM((n, experts, rows), f32),
             pltpu.VMEM((n, rows, cols), bf16),
             pltpu.VMEM((n, half, wide), f32),
             pltpu.VMEM((n, half, wide), bf16),
@@ -293,10 +303,10 @@
             pltpu.VMEM((n, rows, cols), bf16),
             pltpu.VMEM((n, rows, cols), bf16),
             pltpu.VMEM((rows, cols), f32),
-            dma((3,)),
-            dma((2, n)),
-            dma((n,)),
-            dma((n,)),
+            dma((6,)),
+            dma((2 * n - 2,)),
+            dma((n,)),
+            dma((2 * n - 2,)),
             dma((n,)),
             dma((n,)),
             dma((n,)),
@@ -308,9 +318,9 @@
             dma((n,)),
         ],
         compiler_params=pltpu.CompilerParams(
-            collective_id=0, has_side_effects=True, vmem_limit_bytes=48 * 1024 * 1024
+            collective_id=0, has_side_effects=True, vmem_limit_bytes=67043328
         ),
-    )(expert_ids, gate_values, activations, expert_gate, expert_up, expert_down)
+    )(expert_ids.T, gate_values.T, activations, expert_gate, expert_up, expert_down)
 
 
 def shards(activations, expert_ids, gate_values, expert_gate, expert_up, expert_down):

time: 47.3 us -> 46.4 us (0.981)
  local copies, waits for them, and re-layouts: 5.27 us -> 1.57 us
  Pallas kernels: 41.8 us -> 44.6 us
    unnamed x13 -> x1, local copies, waits for them, and re-layouts: 5.27 us -> 1.57 us
    pallas_call x1, Pallas kernels: 41.8 us -> 44.6 us  [dense_layer(): pl.pallas_call(functools.partial(dense_kernel, n), out_shape=jax.ShapeDty...]
where the time goes in v2:
time: 46.4 us; the launch traced here: 46.2 us
  Pallas kernels  44.6 us (96%)
  local copies, waits for them, and re-layouts  1.57 us (3%)
    pallas_call x1, Pallas kernels, dense_layer(): pl.pallas_call(functools.partial(dense_kernel, n), out_shape=jax.ShapeDty...  44.6 us
    unnamed x1, local copies, waits for them, and re-layouts  1.57 us

profile of v2, /device:TPU:0, one launch (start us, length us, event | category | flops | bytes accessed | tf_op | source)
XLA Modules:
  0.0 46.2 jit_solution(18050311125924903493)
XLA Ops:
  0.0 44.6 %shard_map.64 = bf16[128,512]{1,0:T(8,128)(2,1)} custom-call(s32[4,128]{1,0:T(4,128)} %bitcast.2, f32[4,128]{1,0:T(4,128)} %bitcast.3, bf16[128,512]{1,0:T(8,128)(2,1)} %a_hbm.1, bf16[2,512,512]{2,1,0:T(8,128)(2,1)} %wg_hbm.1, bf16[2,512,512]{2,1,0:T(8,128)(2,1)} %wu_hbm.1, bf16[2,512,512]{2,1,0:T(8,128)(2,1)} %wd_hbm.1), custom_call_target="tpu_custom_call" | custom-call | tf_op jit(solution)/shard_map/pallas_call | solution.py:283
  44.6 1.6 %copy.8 = bf16[128,512]{1,0:T(8,128)(2,1)} copy(bf16[128,512]{1,0:T(8,128)(2,1)} %shard_map.64) | data formatting | bytes 262144

commit v3 on v2

--- a/solution.py
+++ b/solution.py
@@ -61,11 +61,11 @@
 
 def run_order(n):
     if n < 4:
-        return [(k, s) for k in "ABCDE" for s in range(n) if (k, s) != ("A", 0)]
+        return [(k, s) for k in "FABCDE" for s in range(n) if s > 0 or k not in "FA"]
     last, middle = n - 1, range(1, n - 2)
-    plan = [("B", 0)]
-    plan += [(k, s) for s in range(1, last) for k in "AB"]
-    plan += [("C", s) for s in range(n - 2)]
+    plan = [("B", 0), ("F", 1)]
+    plan += [(k, s) for s in range(1, last) for k in ("FAB" if s > 1 else "AB")]
+    plan += [("C", 0), ("F", last)] + [("C", s) for s in middle]
     plan += [("A", last), ("B", last)]
     plan += [("D", s) for s in middle] + [("C", n - 2), ("D", 0)] + [("E", s) for s in middle]
     plan += [("C", last), ("D", n - 2), ("E", n - 2), ("E", 0), ("D", last), ("E", last)]
@@ -103,10 +103,10 @@
         for i, (src, dst) in enumerate(
             (
                 (a_hbm, xg.at[me]),
+                (ids_hbm, ids_ref),
+                (gv_hbm, gv_ref),
                 (wg_hbm, wg),
                 (wu_hbm, wu),
-                (ids_hbm, ids_ref),
-                (gv_hbm, gv_ref),
                 (wd_hbm, wd),
             )
         )
@@ -134,7 +134,28 @@
             for i, peer in enumerate(me + d * sign for d in range(1, n) for sign in (1, -1))
         ]
 
-    row_copies, gate_copies = spread(xg, z_send, z_recv), spread(gates, g_send, g_recv)
+    gate_copies = spread(gates, g_send, g_recv)
+    inner = jnp.logical_and(me > 0, me < n - 1)
+    row_copies = [
+        (
+            jnp.logical_and(peer >= 0, peer < n),
+            send(xg.at[me], xg.at[me], z_send.at[0, i], z_recv.at[me], {"exp": lax.rem(peer + n, n)}),
+        )
+        for i, peer in enumerate((me + 1, me - 1))
+    ]
+
+    def onward(s):
+        b = block(s)
+        peer = jnp.where(b < me, me + 1, me - 1)
+        return send(
+            xg.at[b], xg.at[b], z_send.at[1, s], z_recv.at[b], {"exp": lax.rem(peer + n, n)}
+        )
+
+    def hand_rows(s):
+        @pl.when(inner)
+        def _():
+            onward(s).wait_recv()
+            onward(s).start()
 
     def to_core(s):
         return send(csend.at[s], crecv.at[s], c_send.at[s], c_recv.at[s], core_peer)
@@ -163,9 +184,7 @@
     def partial(s):
         b = block(s)
         if s > 0:
-            send(
-                xg.at[b], xg.at[b], z_send.at[0], z_recv.at[b], {"exp": lax.rem(me + 1, n)}
-            ).wait_recv()
+            pl.when(jnp.logical_not(inner))(onward(s).wait_recv)
         first = pl.ds(pl.multiple_of(c * half, half), half)
         second = pl.ds(pl.multiple_of((1 - c) * half, half), half)
         block_rows = jnp.concatenate([xg[b, first, :], xg[b, second, :]], axis=0)
@@ -175,8 +194,7 @@
                 cols = pl.ds((2 * e + i) * ff, ff)
                 csend[s, :, cols] = part[half:].astype(jnp.bfloat16)
                 keep[s, :, cols] = part[:half]
-        if s > 0:
-            to_core(s).start()
+        to_core(s).start()
 
     def chip_sum(s):
         to_core(s).wait_recv()
@@ -228,14 +246,11 @@
             outb[s] = result.astype(jnp.bfloat16)
             result_copy(s).start()
 
-    stages = {"A": partial, "B": chip_sum, "C": activate, "D": hand_on, "E": project}
+    stages = {"A": partial, "B": chip_sum, "C": activate, "D": hand_on, "E": project, "F": hand_rows}
     plan = run_order(n)
     first_projected = next(s for stage, s in plan if stage == "E")
 
     for copy in loads[:3]:
-        copy.wait()
-    partial(0)
-    for copy in loads[3:5]:
         copy.wait()
     experts = lax.broadcasted_iota(jnp.int32, gates.shape[1:], 0)
     table_of_gates = jnp.zeros(gates.shape[1:], jnp.float32)
@@ -243,9 +258,11 @@
         table_of_gates += jnp.where(experts == ids_ref[k : k + 1, :], gv_ref[k : k + 1, :], 0.0)
     gates[me] = table_of_gates
     pl.semaphore_wait(barrier, n + 1)
-    to_core(0).start()
     for condition, copy in row_copies + gate_copies:
         pl.when(condition)(copy.start)
+    for copy in loads[3:5]:
+        copy.wait()
+    partial(0)
     for stage, s in plan:
         stages[stage](s)
 
@@ -267,6 +284,8 @@
             result_copy(s).wait_send()
     for condition, copy in row_copies + gate_copies:
         pl.when(condition)(copy.wait_send)
+    for s in range(1, n):
+        pl.when(inner)(onward(s).wait_send)
 
 
 def dense_layer(activations, expert_ids, gate_values, expert_gate, expert_up, expert_down):
@@ -304,7 +323,7 @@
             pltpu.VMEM((n, rows, cols), bf16),
             pltpu.VMEM((rows, cols), f32),
             dma((6,)),
-            dma((2 * n - 2,)),
+            dma((2, n)),
             dma((n,)),
             dma((2 * n - 2,)),
             dma((n,)),

time: 46.4 us -> 41.4 us (0.89)
  Pallas kernels: 44.6 us -> 39.6 us
    pallas_call x1, Pallas kernels: 44.6 us -> 39.6 us  [dense_layer(): pl.pallas_call(functools.partial(dense_kernel, n), out_shape=jax.ShapeDty...]
where the time goes in v3:
time: 41.4 us; the launch traced here: 41.2 us
  Pallas kernels  39.6 us (96%)
  local copies, waits for them, and re-layouts  1.57 us (4%)
    pallas_call x1, Pallas kernels, dense_layer(): pl.pallas_call(functools.partial(dense_kernel, n), out_shape=jax.ShapeDty...  39.6 us
    unnamed x1, local copies, waits for them, and re-layouts  1.57 us

profile of v3, /device:TPU:0, one launch (start us, length us, event | category | flops | bytes accessed | tf_op | source)
XLA Modules:
  0.0 41.2 jit_solution(17572458933429298438)
XLA Ops:
  0.0 39.6 %shard_map.64 = bf16[128,512]{1,0:T(8,128)(2,1)} custom-call(s32[4,128]{1,0:T(4,128)} %bitcast.2, f32[4,128]{1,0:T(4,128)} %bitcast.3, bf16[128,512]{1,0:T(8,128)(2,1)} %a_hbm.1, bf16[2,512,512]{2,1,0:T(8,128)(2,1)} %wg_hbm.1, bf16[2,512,512]{2,1,0:T(8,128)(2,1)} %wu_hbm.1, bf16[2,512,512]{2,1,0:T(8,128)(2,1)} %wd_hbm.1), custom_call_target="tpu_custom_call" | custom-call | tf_op jit(solution)/shard_map/pallas_call | solution.py:302
  39.6 1.6 %copy.8 = bf16[128,512]{1,0:T(8,128)(2,1)} copy(bf16[128,512]{1,0:T(8,128)(2,1)} %shard_map.64) | data formatting | bytes 262144

commit v4 on v3

--- a/solution.py
+++ b/solution.py
@@ -59,21 +59,25 @@
     return [sorted(range(n), key=lambda b: (abs(b - i), b)) for i in range(n)]
 
 
-def run_order(n):
-    if n < 4:
-        return [(k, s) for k in "FABCDE" for s in range(n) if s > 0 or k not in "FA"]
-    last, middle = n - 1, range(1, n - 2)
-    plan = [("B", 0), ("F", 1)]
-    plan += [(k, s) for s in range(1, last) for k in ("FAB" if s > 1 else "AB")]
-    plan += [("C", 0), ("F", last)] + [("C", s) for s in middle]
-    plan += [("A", last), ("B", last)]
-    plan += [("D", s) for s in middle] + [("C", n - 2), ("D", 0)] + [("E", s) for s in middle]
-    plan += [("C", last), ("D", n - 2), ("E", n - 2), ("E", 0), ("D", last), ("E", last)]
-    return plan
+def run_order(n, pieces):
+    m = n * pieces
+    if n < 4 or pieces != 2:
+        return [(k, s) for k in "FABCDE" for s in range(m) if s >= pieces or k not in "FA"]
+    plan = [("F", 2), ("B", 0), ("F", 4), ("A", 2), ("F", 3), ("B", 1), ("F", 5)]
+    for s in range(3, m - 2):
+        plan += [("F", s)] if s > 5 else []
+        plan += [("A", s), ("B", s - 1)]
+    plan += [("F", m - 2), ("B", m - 3), ("F", m - 1)]
+    plan += [("C", 2), ("A", m - 2), ("C", 3), ("A", m - 1), ("B", m - 2), ("C", 4), ("B", m - 1)]
+    plan += [("C", s) for s in range(5, m - 2)]
+    plan += [(k, s) for s in range(2, m - 4) for k in "DE"]
+    for first, second in ((m - 2, m - 4), (m - 1, m - 3), (0, m - 2), (1, m - 1)):
+        plan += [("C", first), ("D", second), ("E", second)]
+    return plan + [(k, s) for s in range(2) for k in "DE"]
 
 
 def dense_kernel(
-    n, ids_hbm, gv_hbm, a_hbm, wg_hbm, wu_hbm, wd_hbm, out_ref,
+    n, pieces, ids_hbm, gv_hbm, a_hbm, wg_hbm, wu_hbm, wd_hbm, out_ref,
     ids_ref, gv_ref, wg, wu, wd, gates, xg, keep, csend, crecv, mine, xsend, xrecv, hid, outb, ret, acc,
     w_sem, z_send, z_recv, g_send, g_recv, c_send, c_recv, x_send, x_recv, h_send, h_recv,
     r_send, r_recv,
@@ -90,8 +94,11 @@
     def block(step):
         b = me * 0
         for i in range(n):
-            b = jnp.where(me == i, table[i][step], b)
+            b = jnp.where(me == i, table[i][step // pieces], b)
         return b
+
+    def piece(step):
+        return block(step) * pieces + step % pieces
 
     def send(src, dst, ss, rs, where):
         return pltpu.make_async_remote_copy(
@@ -99,10 +106,13 @@
         )
 
     loads = [
-        pltpu.make_async_copy(src, dst, w_sem.at[i])
-        for i, (src, dst) in enumerate(
+        pltpu.make_async_copy(src, dst, w_sem.at[slot])
+        for slot, (src, dst) in enumerate(
             (
-                (a_hbm, xg.at[me]),
+                *(
+                    (a_hbm.at[pl.ds(i * rows, rows)], xg.at[me * pieces + i])
+                    for i in range(pieces)
+                ),
                 (ids_hbm, ids_ref),
                 (gv_hbm, gv_ref),
                 (wg_hbm, wg),
@@ -139,16 +149,21 @@
     row_copies = [
         (
             jnp.logical_and(peer >= 0, peer < n),
-            send(xg.at[me], xg.at[me], z_send.at[0, i], z_recv.at[me], {"exp": lax.rem(peer + n, n)}),
-        )
+            send(
+                xg.at[me * pieces + h], xg.at[me * pieces + h],
+                z_send.at[0, h * 2 + i], z_recv.at[me * pieces + h],
+                {"exp": lax.rem(peer + n, n)},
+            ),
+        )
+        for h in range(pieces)
         for i, peer in enumerate((me + 1, me - 1))
     ]
 
     def onward(s):
         b = block(s)
-        peer = jnp.where(b < me, me + 1, me - 1)
+        peer, p = jnp.where(b < me, me + 1, me - 1), piece(s)
         return send(
-            xg.at[b], xg.at[b], z_send.at[1, s], z_recv.at[b], {"exp": lax.rem(peer + n, n)}
+            xg.at[p], xg.at[p], z_send.at[1, s], z_recv.at[p], {"exp": lax.rem(peer + n, n)}
         )
 
     def hand_rows(s):
@@ -179,11 +194,12 @@
 
     def result_copy(s):
         b = block(s)
-        return send(outb.at[s], ret.at[me], r_send.at[s], r_recv.at[me], {"exp": b})
+        p = me * pieces + s % pieces
+        return send(outb.at[s], ret.at[p], r_send.at[s], r_recv.at[p], {"exp": b})
 
     def partial(s):
-        b = block(s)
-        if s > 0:
+        b = piece(s)
+        if s >= pieces:
             pl.when(jnp.logical_not(inner))(onward(s).wait_recv)
         first = pl.ds(pl.multiple_of(c * half, half), half)
         second = pl.ds(pl.multiple_of((1 - c) * half, half), half)
@@ -206,14 +222,14 @@
 
     def activate(s):
         b = block(s)
-        if s > 0:
+        if s >= pieces and s % pieces == 0:
             send(
                 gates.at[b], gates.at[b], g_send.at[0], g_recv.at[b], {"exp": lax.rem(me + 1, n)}
             ).wait_recv()
         to_chip(s).wait_recv()
-        square = (quarter, rows)
+        square = (quarter, rows * pieces)
         diagonal = lax.broadcasted_iota(jnp.int32, square, 1) == (
-            own_q * quarter + lax.broadcasted_iota(jnp.int32, square, 0)
+            s % pieces * rows + own_q * quarter + lax.broadcasted_iota(jnp.int32, square, 0)
         )
         for e in range(local_experts):
             gate_cols, up_cols = pl.ds(2 * e * ff, ff), pl.ds((2 * e + 1) * ff, ff)
@@ -235,22 +251,22 @@
         hidden_arrival(s, 1).wait_recv()
         hidden_arrival(s, 2).wait_recv()
         if s == first_projected:
-            loads[5].wait()
+            loads[-1].wait()
         h = hid[s].reshape(rows, local_experts * ff)
         result = jnp.dot(
             h, wd[...].reshape(local_experts * ff, wd.shape[2]), preferred_element_type=jnp.float32
         )
-        if s == 0:
-            acc[...] = result
+        if s < pieces:
+            acc[s] = result
         else:
             outb[s] = result.astype(jnp.bfloat16)
             result_copy(s).start()
 
     stages = {"A": partial, "B": chip_sum, "C": activate, "D": hand_on, "E": project, "F": hand_rows}
-    plan = run_order(n)
+    plan = run_order(n, pieces)
     first_projected = next(s for stage, s in plan if stage == "E")
 
-    for copy in loads[:3]:
+    for copy in loads[: pieces + 2]:
         copy.wait()
     experts = lax.broadcasted_iota(jnp.int32, gates.shape[1:], 0)
     table_of_gates = jnp.zeros(gates.shape[1:], jnp.float32)
@@ -260,31 +276,31 @@
     pl.semaphore_wait(barrier, n + 1)
     for condition, copy in row_copies + gate_copies:
         pl.when(condition)(copy.start)
-    for copy in loads[3:5]:
+    for copy in loads[pieces + 2 : -1]:
         copy.wait()
-    partial(0)
+    for h in range(pieces):
+        partial(h)
     for stage, s in plan:
         stages[stage](s)
 
-    total = acc[...]
-    for s in range(1, n):
-        b = block(s)
-        send(
-            outb.at[s], ret.at[b], r_send.at[s], r_recv.at[b], {"exp": b}
-        ).wait_recv()
-        total += ret[b].astype(jnp.float32)
-    out_ref[...] = total.astype(out_ref.dtype)
-
-    for s in range(n):
+    for h in range(pieces):
+        total = acc[h]
+        for s in range(pieces + h, n * pieces, pieces):
+            b, p = block(s), piece(s)
+            send(outb.at[s], ret.at[p], r_send.at[s], r_recv.at[p], {"exp": b}).wait_recv()
+            total += ret[p].astype(jnp.float32)
+        out_ref[h * rows : (h + 1) * rows, :] = total.astype(out_ref.dtype)
+
+    for s in range(n * pieces):
         to_core(s).wait_send()
         to_chip(s).wait_send()
         for kind in range(3):
             hidden_copy(s, kind).wait_send()
-        if s > 0:
+        if s >= pieces:
             result_copy(s).wait_send()
     for condition, copy in row_copies + gate_copies:
         pl.when(condition)(copy.wait_send)
-    for s in range(1, n):
+    for s in range(pieces, n * pieces):
         pl.when(inner)(onward(s).wait_send)
 
 
@@ -293,14 +309,16 @@
     rows, cols = activations.shape
     local_experts, _, ff = expert_gate.shape
     wide, joined = 2 * local_experts * ff, local_experts * ff
-    half, quarter = rows // 2, rows // 4
+    pieces = 2 if rows % 128 == 0 else 1
+    part = rows // pieces
+    half, quarter, steps = part // 2, part // 4, n * pieces
     experts = -(-local_experts * n // 8) * 8
     top = expert_ids.shape[1]
     bf16, f32 = jnp.bfloat16, jnp.float32
     vmem, hbm = pl.BlockSpec(memory_space=pltpu.VMEM), pl.BlockSpec(memory_space=pltpu.HBM)
     dma = pltpu.SemaphoreType.DMA
     return pl.pallas_call(
-        functools.partial(dense_kernel, n),
+        functools.partial(dense_kernel, n, pieces),
         out_shape=jax.ShapeDtypeStruct((rows, cols), bf16),
         in_specs=[hbm] * 6,
         out_specs=vmem,
@@ -311,30 +329,30 @@
             pltpu.VMEM(expert_up.shape, bf16),
             pltpu.VMEM(expert_down.shape, bf16),
             pltpu.VMEM((n, experts, rows), f32),
-            pltpu.VMEM((n, rows, cols), bf16),
-            pltpu.VMEM((n, half, wide), f32),
-            pltpu.VMEM((n, half, wide), bf16),
-            pltpu.VMEM((n, half, wide), bf16),
-            pltpu.VMEM((n, quarter, wide), f32),
-            pltpu.VMEM((n, quarter, wide), bf16),
-            pltpu.VMEM((n, quarter, wide), bf16),
-            pltpu.VMEM((n, 4, quarter, joined), bf16),
-            pltpu.VMEM((n, rows, cols), bf16),
-            pltpu.VMEM((n, rows, cols), bf16),
-            pltpu.VMEM((rows, cols), f32),
-            dma((6,)),
-            dma((2, n)),
-            dma((n,)),
+            pltpu.VMEM((steps, part, cols), bf16),
+            pltpu.VMEM((steps, half, wide), f32),
+            pltpu.VMEM((steps, half, wide), bf16),
+            pltpu.VMEM((steps, half, wide), bf16),
+            pltpu.VMEM((steps, quarter, wide), f32),
+            pltpu.VMEM((steps, quarter, wide), bf16),
+            pltpu.VMEM((steps, quarter, wide), bf16),
+            pltpu.VMEM((steps, 4, quarter, joined), bf16),
+            pltpu.VMEM((steps, part, cols), bf16),
+            pltpu.VMEM((steps, part, cols), bf16),
+            pltpu.VMEM((pieces, part, cols), f32),
+            dma((5 + pieces,)),
+            dma((2, steps)),
+            dma((steps,)),
             dma((2 * n - 2,)),
-            dma((n,)),
-            dma((n,)),
-            dma((n,)),
-            dma((n,)),
-            dma((n,)),
-            dma((n, 3)),
-            dma((n, 3)),
-            dma((n,)),
-            dma((n,)),
+            dma((steps,)),
+            dma((steps,)),
+            dma((steps,)),
+            dma((steps,)),
+            dma((steps,)),
+            dma((steps, 3)),
+            dma((steps, 3)),
+            dma((steps,)),
+            dma((steps,)),
         ],
         compiler_params=pltpu.CompilerParams(
             collective_id=0, has_side_effects=True, vmem_limit_bytes=67043328

time: 41.4 us -> 39.2 us (0.947)
  Pallas kernels: 39.6 us -> 37.5 us
    pallas_call x1, Pallas kernels: 39.6 us -> 37.5 us  [dense_layer(): pl.pallas_call(functools.partial(dense_kernel, n, pieces), out_shape=jax....]
where the time goes in v4:
time: 39.2 us; the launch traced here: 39.1 us
  Pallas kernels  37.5 us (96%)
  local copies, waits for them, and re-layouts  1.57 us (4%)
    pallas_call x1, Pallas kernels, dense_layer(): pl.pallas_call(functools.partial(dense_kernel, n, pieces), out_shape=jax....  37.5 us
    unnamed x1, local copies, waits for them, and re-layouts  1.57 us

profile of v4, /device:TPU:0, one launch (start us, length us, event | category | flops | bytes accessed | tf_op | source)
XLA Modules:
  0.0 39.1 jit_solution(10973927098590599228)
XLA Ops:
  0.0 37.5 %shard_map.64 = bf16[128,512]{1,0:T(8,128)(2,1)} custom-call(s32[4,128]{1,0:T(4,128)} %bitcast.2, f32[4,128]{1,0:T(4,128)} %bitcast.3, bf16[128,512]{1,0:T(8,128)(2,1)} %a_hbm.1, bf16[2,512,512]{2,1,0:T(8,128)(2,1)} %wg_hbm.1, bf16[2,512,512]{2,1,0:T(8,128)(2,1)} %wu_hbm.1, bf16[2,512,512]{2,1,0:T(8,128)(2,1)} %wd_hbm.1), custom_call_target="tpu_custom_call" | custom-call | tf_op jit(solution)/shard_map/pallas_call | solution.py:320
  37.5 1.6 %copy.8 = bf16[128,512]{1,0:T(8,128)(2,1)} copy(bf16[128,512]{1,0:T(8,128)(2,1)} %shard_map.64) | data formatting | bytes 262144

commit v5 on v4

--- a/solution.py
+++ b/solution.py
@@ -121,9 +121,6 @@
             )
         )
     ]
-    for copy in loads:
-        copy.start()
-
     barrier = pltpu.get_barrier_semaphore()
     for j in range(1, n):
         pl.semaphore_signal(
@@ -131,6 +128,9 @@
         )
     for peer in (core_peer, chip_peer):
         pl.semaphore_signal(barrier, inc=1, device_id=peer, device_id_type=MESH)
+
+    for copy in loads:
+        copy.start()
 
     def spread(buffer, send_sem, recv_sem):
         return [

time: 39.2 us -> 39.2 us (level)
  no operation moved by 1% of the time
where the time goes in v5:
time: 39.2 us; the launch traced here: 39.1 us
  Pallas kernels  37.5 us (96%)
  local copies, waits for them, and re-layouts  1.57 us (4%)
    pallas_call x1, Pallas kernels, dense_layer(): pl.pallas_call(functools.partial(dense_kernel, n, pieces), out_shape=jax....  37.5 us
    unnamed x1, local copies, waits for them, and re-layouts  1.57 us

profile of v5, /device:TPU:0, one launch (start us, length us, event | category | flops | bytes accessed | tf_op | source)
XLA Modules:
  0.0 39.1 jit_solution(4413106275989409050)
XLA Ops:
  0.0 37.5 %shard_map.64 = bf16[128,512]{1,0:T(8,128)(2,1)} custom-call(s32[4,128]{1,0:T(4,128)} %bitcast.2, f32[4,128]{1,0:T(4,128)} %bitcast.3, bf16[128,512]{1,0:T(8,128)(2,1)} %a_hbm.1, bf16[2,512,512]{2,1,0:T(8,128)(2,1)} %wg_hbm.1, bf16[2,512,512]{2,1,0:T(8,128)(2,1)} %wu_hbm.1, bf16[2,512,512]{2,1,0:T(8,128)(2,1)} %wd_hbm.1), custom_call_target="tpu_custom_call" | custom-call | tf_op jit(solution)/shard_map/pallas_call | solution.py:320
  37.5 1.6 %copy.8 = bf16[128,512]{1,0:T(8,128)(2,1)} copy(bf16[128,512]{1,0:T(8,128)(2,1)} %shard_map.64) | data formatting | bytes 262144
